TPU v7x, 256 devices: a whole 4x4x8 slice. The times are simulated.
256 devices in a mesh: ctx: 32 (over z_hi, x, core), tp: 8 (over y, z_lo).
Axes of the slice: x: 4, y: 4, z: 8 (z_hi: 4, z_lo: 2; z = z_hi * 2 + z_lo), core: 2. Of those that a mesh axis runs over, the one named last changes fastest.
Arguments:
- features: bfloat16 [16384, 3, 4096], P('ctx', None, 'tp'), may hold values from -6 to 6
- short_filter: float32 [3, 7, 4096], P(None, None, 'tp'), may hold values from -2 to 2
- decay_rate: float32 [16, 4096], P(None, 'tp'), may hold values from 0 to 1, as said below
- residue: float32 [16, 4096], P(None, 'tp'), may hold values from -2 to 2
- skip_gain: float32 [4096], P('tp'), may hold values from -4 to 4
- norm_gain: float32 [4096], replicated, may hold values from 0.1 to 1.9
- qkv_weight: bfloat16 [4096, 3, 2048], P('ctx', None, 'tp'), may hold values from -2 to 2
Outputs:
- mixer: bfloat16 [16384, 4096], P('ctx', 'tp')
- attended: bfloat16 [16384, 2048], P('ctx', 'tp')
Inputs may be any that keep to these rules, and one draw needn't show every extreme that they name: `decay_rate`: decay rates are positive.
All inputs are finite; a program needn't handle non-finite values.
Results may differ from a plain program's by a relative error of at most 0.01.
Values may be sent and summed in bfloat16 or wider, within the bound.
No kernel may reach another device: no remote copies, remote signals or barrier semaphores. Data moves between devices by JAX's collectives and lax.ppermute only.
A program may use at most 128 MiB of HBM per device.

v0:
```python
from functools import reduce
import math

import jax
import jax.numpy as jnp
from jax import lax
from jax.sharding import PartitionSpec as P

HD = 128
TAPS = 7
WINDOW = 3


EPSILON = 1e-06
PRECISE = lax.Precision.HIGHEST


def from_behind(value, axis, steps):
    count = lax.axis_size(axis)
    leading, last = (max(0, -steps), min(count, count - steps))
    return lax.ppermute(value, axis, [(source, source + steps) for source in range(leading, last)])


def modal_toeplitz(mixing, decay, block_len):
    distance = jnp.arange(block_len)[:, None] - jnp.arange(block_len)[None, :]
    lag_float = jnp.maximum(distance, 0).astype(jnp.float32)
    channels = mixing.shape[1]
    start = jnp.zeros((channels, block_len, block_len), jnp.float32)

    def add_mode(mode, running):
        weight_row = lax.dynamic_index_in_dim(mixing, mode, 0, keepdims=False)
        rate_row = lax.dynamic_index_in_dim(decay, mode, 0, keepdims=False)
        term = weight_row[:, None, None] * jnp.exp(-rate_row[:, None, None] * lag_float[None])
        return running + term

    summed = lax.fori_loop(0, mixing.shape[0], add_mode, start)
    return jnp.where(distance[None] >= 0, summed, 0.0)


def channel_conv(signal, decay, residue, skip_gain):
    channels, length = signal.shape
    block_len = math.gcd(length, 256)
    block_count = length // block_len
    blocked = signal.reshape(channels, block_count, block_len)
    rate_cols = decay.T
    mode_weights = residue * jnp.sqrt(decay)
    mixing = mode_weights.T
    offsets = jnp.arange(block_len).astype(jnp.float32)
    trailing = jnp.exp(-rate_cols[:, :, None] * (block_len - 1.0 - offsets)[None, None, :])
    block_ends = jnp.einsum("cbs,cns->cnb", blocked, trailing, precision=PRECISE)
    block_ids = jnp.arange(block_count)
    spacing = block_ids[:, None] - 1 - block_ids[None, :]
    powers = (block_len * jnp.maximum(spacing, 0)).astype(jnp.float32)
    carry = jnp.where(
        spacing[None, None] >= 0, jnp.exp(-rate_cols[:, :, None, None] * powers[None, None]), 0.0
    )
    entering = jnp.einsum("cnkb,cnb->cnk", carry, block_ends, precision=PRECISE)
    leading = jnp.exp(-rate_cols[:, :, None] * (offsets + 1.0)[None, None, :])
    across = jnp.einsum("cnk,cns->cks", entering * mixing[:, :, None], leading, precision=PRECISE)
    toeplitz = modal_toeplitz(mode_weights, decay, block_len)
    within = jnp.einsum("cts,cbs->cbt", toeplitz, blocked, precision=PRECISE)
    return (within + across + skip_gain[:, None, None] * blocked).reshape(channels, length)


def on_device(features, short_filter, decay_rate, residue, skip_gain, norm_gain, qkv_weight):
    tok_dev, _, channels = features.shape
    rim_rows = features[tok_dev - (TAPS - 1) :]
    before = from_behind(rim_rows, "ctx", 1)
    extended = jnp.concatenate([before, features], axis=0).astype(jnp.float32)
    short_conv = jnp.zeros((tok_dev, 3, channels), jnp.float32)
    for offset in range(TAPS):
        first_row = TAPS - 1 - offset
        short_conv = (
            short_conv
            + short_filter[:, offset, :][None] * extended[first_row : first_row + tok_dev]
        )
    gated = (short_conv[:, 1] * short_conv[:, 2]).astype(jnp.bfloat16)
    per_device = channels // lax.axis_size("ctx")
    by_channel = lax.all_to_all(gated.T, "ctx", split_axis=0, concat_axis=1, tiled=True)
    first_channel = lax.axis_index("ctx") * per_device
    decay_part = lax.dynamic_slice_in_dim(decay_rate, first_channel, per_device, 1)
    residue_part = lax.dynamic_slice_in_dim(residue, first_channel, per_device, 1)
    skip_part = lax.dynamic_slice_in_dim(skip_gain, first_channel, per_device, 0)
    filtered = channel_conv(
        by_channel.astype(jnp.float32), decay_part, residue_part, skip_part
    ).astype(jnp.bfloat16)
    long_part = lax.all_to_all(filtered, "ctx", split_axis=1, concat_axis=0, tiled=True).T
    mixer = (short_conv[:, 0] * long_part.astype(jnp.float32)).astype(jnp.bfloat16)
    gathered = lax.all_gather(mixer, "tp", axis=1, tiled=True)
    as_float = gathered.astype(jnp.float32)
    inverse = lax.rsqrt(jnp.mean(as_float * as_float, axis=1, keepdims=True) + EPSILON)
    normed = (as_float * inverse * norm_gain[None]).astype(jnp.bfloat16)
    head_cols = qkv_weight.shape[2]
    shard_rows = lax.all_gather(qkv_weight, "ctx", axis=0, tiled=True)
    flat_rows = shard_rows.reshape(shard_rows.shape[0], 3 * head_cols)
    projected = jnp.dot(normed, flat_rows, preferred_element_type=jnp.float32).astype(jnp.bfloat16)
    heads = head_cols // HD
    query = projected[:, :head_cols].reshape(tok_dev, heads, HD)
    kv_pair = projected[:, head_cols:]
    blocks_kv = [kv_pair]
    for lag_step in range(WINDOW - 1):
        blocks_kv.append(from_behind(blocks_kv[-1], "ctx", 1))
    position = lax.axis_index("ctx")
    row_ids = jnp.arange(tok_dev)
    causal = row_ids[:, None] >= row_ids[None, :]
    score_list = []
    for lag_step in range(WINDOW):
        keys = blocks_kv[lag_step][:, :head_cols].reshape(tok_dev, heads, HD)
        scores = jnp.einsum(
            "thd,shd->hts", query, keys, preferred_element_type=jnp.float32
        ) / math.sqrt(HD)
        if lag_step == 0:
            allowed = causal
        else:
            allowed = jnp.broadcast_to(position >= lag_step, causal.shape)
        score_list.append(jnp.where(allowed[None], scores, -jnp.inf))
    peak = reduce(jnp.maximum, [jnp.max(entry, axis=2) for entry in score_list])
    total = jnp.zeros((heads, tok_dev), jnp.float32)
    output = jnp.zeros((tok_dev, heads, HD), jnp.float32)
    for lag_step in range(WINDOW):
        expo = jnp.exp(score_list[lag_step] - peak[:, :, None])
        total = total + jnp.sum(expo, axis=2)
        values = blocks_kv[lag_step][:, head_cols:].reshape(tok_dev, heads, HD)
        output = output + jnp.einsum(
            "hts,shd->thd", expo.astype(jnp.bfloat16), values, preferred_element_type=jnp.float32
        )
    attended = (output / total.T[:, :, None]).astype(jnp.bfloat16).reshape(tok_dev, head_cols)
    return (mixer, attended)


def solution(mesh):
    placed = (
        P("ctx", None, "tp"),
        P(None, None, "tp"),
        P(None, "tp"),
        P(None, "tp"),
        P("tp"),
        P(),
        P("ctx", None, "tp"),
    )
    return jax.shard_map(
        on_device,
        mesh=mesh,
        in_specs=placed,
        out_specs=(P("ctx", "tp"), P("ctx", "tp")),
        check_vma=False,
    )
```

profile of v0, /device:TPU:128, one launch (start us, length us, event | category | flops | bytes accessed | tf_op | source)
XLA Modules:
  0.0 409.7 jit_solution(15432068327113039703)
XLA Ops:
  13.4 79.2 %while.14 = (s32[]{:T(128)}, f32[16,256,256]{2,1,0:T(8,128)}, f32[16,16]{1,0:T(8,128)S(1)}, f32[16,16]{1,0:T(8,128)S(1)}, s32[]{:T(128)}, /*index=5*/s32[]{:T(128)}) while((s32[]{:T(128)}, f32[16,256,256]{2,1,0:T(8,128)}, f32[16,16]{1,0:T(8,128)S(1)}, f32[16,16]{1,0:T(8,128)S(1)}, s32[]{:T(128)}, /*index=5*/s32[]{:T(128)}) %tuple.60), condition=%wide.region_1.2_spmd.clone, body=%wide.region_0.1_spmd.clone.sunk | while | flops 4390931 | bytes 8913363 | solution.py:36
  16.4 5.0 %select_add_fusion.2 = f32[16,256,256]{2,1,0:T(8,128)} fusion(f32[16,256,256]{2,1,0:T(8,128)} %get-tuple-element.195, f32[256,256]{1,0:T(8,128)S(1)} %maximum_convert_fusion.3, f32[16]{0:T(128)S(1)} %get-tuple-element.186, f32[16]{0:T(128)S(1)} %get-tuple-element.187, pred[]{:T(512)S(6)} %compare.3), kind=kLoop, calls=%fused_computation.1.clone.1 | loop fusion | flops 4194304 | bytes 8650881 | tf_op jit(solution)/shard_map/while/body/eval_jaxpr/add | solution.py:34
  21.5 5.0 %select_add_fusion.2 = f32[16,256,256]{2,1,0:T(8,128)} fusion(f32[16,256,256]{2,1,0:T(8,128)} %get-tuple-element.195, f32[256,256]{1,0:T(8,128)S(1)} %maximum_convert_fusion.3, f32[16]{0:T(128)S(1)} %get-tuple-element.186, f32[16]{0:T(128)S(1)} %get-tuple-element.187, pred[]{:T(512)S(6)} %compare.3), kind=kLoop, calls=%fused_computation.1.clone.1 | loop fusion | flops 4194304 | bytes 8650881 | tf_op jit(solution)/shard_map/while/body/eval_jaxpr/add | solution.py:34
  26.5 5.0 %select_add_fusion.2 = f32[16,256,256]{2,1,0:T(8,128)} fusion(f32[16,256,256]{2,1,0:T(8,128)} %get-tuple-element.195, f32[256,256]{1,0:T(8,128)S(1)} %maximum_convert_fusion.3, f32[16]{0:T(128)S(1)} %get-tuple-element.186, f32[16]{0:T(128)S(1)} %get-tuple-element.187, pred[]{:T(512)S(6)} %compare.3), kind=kLoop, calls=%fused_computation.1.clone.1 | loop fusion | flops 4194304 | bytes 8650881 | tf_op jit(solution)/shard_map/while/body/eval_jaxpr/add | solution.py:34
  31.6 5.0 %select_add_fusion.2 = f32[16,256,256]{2,1,0:T(8,128)} fusion(f32[16,256,256]{2,1,0:T(8,128)} %get-tuple-element.195, f32[256,256]{1,0:T(8,128)S(1)} %maximum_convert_fusion.3, f32[16]{0:T(128)S(1)} %get-tuple-element.186, f32[16]{0:T(128)S(1)} %get-tuple-element.187, pred[]{:T(512)S(6)} %compare.3), kind=kLoop, calls=%fused_computation.1.clone.1 | loop fusion | flops 4194304 | bytes 8650881 | tf_op jit(solution)/shard_map/while/body/eval_jaxpr/add | solution.py:34
  36.7 5.0 %select_add_fusion.2 = f32[16,256,256]{2,1,0:T(8,128)} fusion(f32[16,256,256]{2,1,0:T(8,128)} %get-tuple-element.195, f32[256,256]{1,0:T(8,128)S(1)} %maximum_convert_fusion.3, f32[16]{0:T(128)S(1)} %get-tuple-element.186, f32[16]{0:T(128)S(1)} %get-tuple-element.187, pred[]{:T(512)S(6)} %compare.3), kind=kLoop, calls=%fused_computation.1.clone.1 | loop fusion | flops 4194304 | bytes 8650881 | tf_op jit(solution)/shard_map/while/body/eval_jaxpr/add | solution.py:34
  41.8 5.0 %select_add_fusion.2 = f32[16,256,256]{2,1,0:T(8,128)} fusion(f32[16,256,256]{2,1,0:T(8,128)} %get-tuple-element.195, f32[256,256]{1,0:T(8,128)S(1)} %maximum_convert_fusion.3, f32[16]{0:T(128)S(1)} %get-tuple-element.186, f32[16]{0:T(128)S(1)} %get-tuple-element.187, pred[]{:T(512)S(6)} %compare.3), kind=kLoop, calls=%fused_computation.1.clone.1 | loop fusion | flops 4194304 | bytes 8650881 | tf_op jit(solution)/shard_map/while/body/eval_jaxpr/add | solution.py:34
  46.9 5.0 %select_add_fusion.2 = f32[16,256,256]{2,1,0:T(8,128)} fusion(f32[16,256,256]{2,1,0:T(8,128)} %get-tuple-element.195, f32[256,256]{1,0:T(8,128)S(1)} %maximum_convert_fusion.3, f32[16]{0:T(128)S(1)} %get-tuple-element.186, f32[16]{0:T(128)S(1)} %get-tuple-element.187, pred[]{:T(512)S(6)} %compare.3), kind=kLoop, calls=%fused_computation.1.clone.1 | loop fusion | flops 4194304 | bytes 8650881 | tf_op jit(solution)/shard_map/while/body/eval_jaxpr/add | solution.py:34
  52.0 5.0 %select_add_fusion.2 = f32[16,256,256]{2,1,0:T(8,128)} fusion(f32[16,256,256]{2,1,0:T(8,128)} %get-tuple-element.195, f32[256,256]{1,0:T(8,128)S(1)} %maximum_convert_fusion.3, f32[16]{0:T(128)S(1)} %get-tuple-element.186, f32[16]{0:T(128)S(1)} %get-tuple-element.187, pred[]{:T(512)S(6)} %compare.3), kind=kLoop, calls=%fused_computation.1.clone.1 | loop fusion | flops 4194304 | bytes 8650881 | tf_op jit(solution)/shard_map/while/body/eval_jaxpr/add | solution.py:34
  57.0 5.0 %select_add_fusion.2 = f32[16,256,256]{2,1,0:T(8,128)} fusion(f32[16,256,256]{2,1,0:T(8,128)} %get-tuple-element.195, f32[256,256]{1,0:T(8,128)S(1)} %maximum_convert_fusion.3, f32[16]{0:T(128)S(1)} %get-tuple-element.186, f32[16]{0:T(128)S(1)} %get-tuple-element.187, pred[]{:T(512)S(6)} %compare.3), kind=kLoop, calls=%fused_computation.1.clone.1 | loop fusion | flops 4194304 | bytes 8650881 | tf_op jit(solution)/shard_map/while/body/eval_jaxpr/add | solution.py:34
  62.1 5.0 %select_add_fusion.2 = f32[16,256,256]{2,1,0:T(8,128)} fusion(f32[16,256,256]{2,1,0:T(8,128)} %get-tuple-element.195, f32[256,256]{1,0:T(8,128)S(1)} %maximum_convert_fusion.3, f32[16]{0:T(128)S(1)} %get-tuple-element.186, f32[16]{0:T(128)S(1)} %get-tuple-element.187, pred[]{:T(512)S(6)} %compare.3), kind=kLoop, calls=%fused_computation.1.clone.1 | loop fusion | flops 4194304 | bytes 8650881 | tf_op jit(solution)/shard_map/while/body/eval_jaxpr/add | solution.py:34
  67.2 5.0 %select_add_fusion.2 = f32[16,256,256]{2,1,0:T(8,128)} fusion(f32[16,256,256]{2,1,0:T(8,128)} %get-tuple-element.195, f32[256,256]{1,0:T(8,128)S(1)} %maximum_convert_fusion.3, f32[16]{0:T(128)S(1)} %get-tuple-element.186, f32[16]{0:T(128)S(1)} %get-tuple-element.187, pred[]{:T(512)S(6)} %compare.3), kind=kLoop, calls=%fused_computation.1.clone.1 | loop fusion | flops 4194304 | bytes 8650881 | tf_op jit(solution)/shard_map/while/body/eval_jaxpr/add | solution.py:34
  72.3 5.0 %select_add_fusion.2 = f32[16,256,256]{2,1,0:T(8,128)} fusion(f32[16,256,256]{2,1,0:T(8,128)} %get-tuple-element.195, f32[256,256]{1,0:T(8,128)S(1)} %maximum_convert_fusion.3, f32[16]{0:T(128)S(1)} %get-tuple-element.186, f32[16]{0:T(128)S(1)} %get-tuple-element.187, pred[]{:T(512)S(6)} %compare.3), kind=kLoop, calls=%fused_computation.1.clone.1 | loop fusion | flops 4194304 | bytes 8650881 | tf_op jit(solution)/shard_map/while/body/eval_jaxpr/add | solution.py:34
  87.5 5.0 %select_add_fusion.2 = f32[16,256,256]{2,1,0:T(8,128)} fusion(f32[16,256,256]{2,1,0:T(8,128)} %get-tuple-element.195, f32[256,256]{1,0:T(8,128)S(1)} %maximum_convert_fusion.3, f32[16]{0:T(128)S(1)} %get-tuple-element.186, f32[16]{0:T(128)S(1)} %get-tuple-element.187, pred[]{:T(512)S(6)} %compare.3), kind=kLoop, calls=%fused_computation.1.clone.1 | loop fusion | flops 4194304 | bytes 8650881 | tf_op jit(solution)/shard_map/while/body/eval_jaxpr/add | solution.py:34
  96.8 7.0 %fusion.19 = f32[512,3,512]{0,2,1:T(8,128)S(1)} fusion(f32[518,3,512]{0,2,1:T(8,128)S(1)} %maximum_convert_fusion.1, f32[3,512]{1,0:T(4,128)S(1)} %copy-done.6, f32[3,512]{1,0:T(4,128)S(1)} %copy-done.7, f32[3,512]{1,0:T(4,128)S(1)} %copy-done.8, f32[3,512]{1,0:T(4,128)S(1)} %copy-done.9, f32[3,512]{1,0:T(4,128)S(1)} %copy-done.10, ...), kind=kLoop, calls=%fused_computation.24 | loop fusion | flops 10223616 | bytes 25208832 | tf_op jit(solution)/shard_map/add | solution.py:74
  104.8 10.8 %all-to-all-start = ((bf16[32,16,512]{2,1,0:T(8,128)(2,1)}), bf16[32,16,512]{2,1,0:T(8,128)(2,1)}, u32[]{:S(2)}, u32[]{:S(2)}) async-start(bf16[32,16,512]{2,1,0:T(8,128)(2,1)} %bitcast.103), calls=%async_computation | async-start | bytes 1048576 | tf_op jit(solution)/shard_map/all_to_all | solution.py:79
  117.0 13.6 %all-to-all-done = bf16[32,16,512]{2,1,0:T(8,128)(2,1)} async-done(((bf16[32,16,512]{2,1,0:T(8,128)(2,1)}), bf16[32,16,512]{2,1,0:T(8,128)(2,1)}, u32[]{:S(2)}, u32[]{:S(2)}) %all-to-all-start) | async-done | bytes 524320 | tf_op jit(solution)/shard_map/all_to_all | solution.py:79
  136.3 14.1 %fusion.5 = f32[16,16,1,64]{3,2,1,0:T(1,128)S(1)} fusion(f32[16,16,64,1]{2,3,1,0:T(1,128)S(1)} %bitcast.108, f32[64,64]{1,0:T(8,128)S(1)} %multiply_convert_fusion, f32[16,16]{1,0:T(8,128)S(1)} %copy.30, pred[64,64]{1,0:T(8,128)(4,1)S(1)} %fusion.97), kind=kOutput, calls=%fused_computation.10 | convolution fusion | flops 14680064 | bytes 152576 | tf_op jit(solution)/shard_map/cnkb,cnb->cnk/dot_general | solution.py:57
  158.4 21.9 %all_to_all.26 = bf16[16,32,512]{2,0,1:T(8,128)(2,1)S(1)} all-to-all(bf16[16,32,512]{2,0,1:T(8,128)(2,1)S(1)} %copy.33), channel_id=1, replica_groups=mesh['ctx'=32,'tp'=8] {'ctx'}, dimensions={1} | all-to-all | bytes 1048576 | tf_op jit(solution)/shard_map/all_to_all | solution.py:87
  184.3 89.4 %all-gather.3.cloned.1.call-done = bf16[512,4096]{0,1:T(8,128)(2,1)} async-done(((bf16[512,512]{0,1:T(8,128)(2,1)}), bf16[512,4096]{0,1:T(8,128)(2,1)}) %all-gather.3.cloned.1.call-update) | async-done | bytes 4194320 | tf_op jit(solution)/shard_map/all_gather | solution.py:89
  276.9 71.4 %all-gather.5.cloned.1.call-done = bf16[4096,3,256]{0,2,1:T(8,128)(2,1)} async-done(((bf16[128,3,256]{0,2,1:T(8,128)(2,1)}), bf16[4096,3,256]{0,2,1:T(8,128)(2,1)}) %all-gather.5.cloned.1.call-update) | async-done | bytes 6291472 | tf_op jit(solution)/shard_map/all_gather | solution.py:94
  348.3 8.2 %fusion.36 = bf16[512,768]{1,0:T(8,128)(2,1)S(1)} fusion(bf16[4096,768]{0,1:T(8,128)(2,1)} %bitcast.112, bf16[512,4096]{0,1:T(8,128)(2,1)} %all-gather.3.cloned.1.call-done, f32[4096]{0:T(1024)S(1)} %copy-done.12, f32[512]{0:T(512)S(1)} %add_rsqrt_fusion), kind=kOutput, calls=%fused_computation.54 | convolution fusion | flops 3230007296 | bytes 11290624 | tf_op jit(solution)/shard_map/dot_general | solution.py:96
  361.5 11.9 %collective-permute-done.1 = bf16[512,512]{1,0:T(8,128)(2,1)} collective-permute-done((bf16[512,512]{1,0:T(8,128)(2,1)S(1)}, bf16[512,512]{1,0:T(8,128)(2,1)}, u32[]{:S(2)}, u32[]{:S(2)}) %collective-permute-start.1) | collective-permute-done | bytes 524320 | tf_op jit(solution)/shard_map/ppermute | solution.py:21
  377.3 16.9 %collective-permute-done.2 = bf16[512,512]{1,0:T(8,128)(2,1)} collective-permute-done((bf16[512,512]{1,0:T(8,128)(2,1)}, bf16[512,512]{1,0:T(8,128)(2,1)}, u32[]{:S(2)}, u32[]{:S(2)}) %collective-permute-start.2) | collective-permute-done | bytes 524320 | tf_op jit(solution)/shard_map/ppermute | solution.py:21
  (121 shorter events, 64.4 us)
Async XLA Ops:
  8.9 87.0 %collective-permute-start = (bf16[6,3,512]{0,2,1:T(8,128)(2,1)}, bf16[6,3,512]{0,2,1:T(8,128)(2,1)S(1)}, u32[]{:S(2)}, u32[]{:S(2)}) collective-permute-start(bf16[6,3,512]{0,2,1:T(8,128)(2,1)} %copy.27), channel_id=1, source_target_pairs={{0,8},{8,16},{16,24},{24,32},{32,40},{40,48},{48,56},{56,64},{64,7... | collective-permute-start | bytes 55304 | tf_op jit(solution)/shard_map/ppermute | solution.py:21
  13.4 81.0 %copy-start.3 = (bf16[512,3,512]{2,0,1:T(8,128)(2,1)S(1)}, bf16[512,3,512]{2,0,1:T(8,128)(2,1)}, u32[]{:S(2)}) copy-start(bf16[512,3,512]{2,0,1:T(8,128)(2,1)} %param.9) | copy-start | bytes 4718596
  95.1 1.7 copy-start.6
  95.1 1.7 copy-start.7
  95.1 1.7 copy-start.8
  95.1 1.7 copy-start.9
  95.2 1.7 copy-start.10
  95.2 1.7 copy-start.11
  104.8 25.7 %all-to-all-start = ((bf16[32,16,512]{2,1,0:T(8,128)(2,1)}), bf16[32,16,512]{2,1,0:T(8,128)(2,1)}, u32[]{:S(2)}, u32[]{:S(2)}) async-start(bf16[32,16,512]{2,1,0:T(8,128)(2,1)} %bitcast.103), calls=%async_computation | async-start | bytes 1048576 | tf_op jit(solution)/shard_map/all_to_all | solution.py:79
  115.6 158.1 %all-gather.3.cloned.1.call-start = ((), (), s32[]{:S(2)}) async-start(), calls=%async_computation.2 | async-start | bytes 4718592 | tf_op jit(solution)/shard_map/all_gather | solution.py:89
  136.3 15.4 %copy-start = (f32[16,256,256]{2,1,0:T(8,128)S(1)}, f32[16,256,256]{2,1,0:T(8,128)}, u32[]{:S(2)}) copy-start(f32[16,256,256]{2,1,0:T(8,128)} %get-tuple-element.96) | copy-start | bytes 12582916
  136.3 15.4 %copy-start.1 = (bf16[16,64,256]{2,1,0:T(8,128)(2,1)S(1)}, bf16[16,64,256]{2,1,0:T(8,128)(2,1)}, u32[]{:S(2)}) copy-start(bf16[16,64,256]{2,1,0:T(8,128)(2,1)} %reshape.174) | copy-start | bytes 1572868
  155.0 26.3 %copy-start.5 = (bf16[128,3,256]{2,0,1:T(8,128)(2,1)S(1)}, bf16[128,3,256]{2,0,1:T(8,128)(2,1)}, u32[]{:S(2)}) copy-start(bf16[128,3,256]{2,0,1:T(8,128)(2,1)} %param.15) | copy-start | bytes 589828
  181.3 167.0 %copy-start.12 = (f32[4096]{0:T(1024)S(1)}, f32[4096]{0:T(1024)}, u32[]{:S(2)}) copy-start(f32[4096]{0:T(1024)} %param.14) | copy-start | bytes 49156
  181.3 167.0 %all-gather.5.cloned.1.call-start = ((), (), s32[]{:S(2)}) async-start(), calls=%async_computation.3 | async-start | bytes 6488064 | tf_op jit(solution)/shard_map/all_gather | solution.py:94
  356.5 16.9 %collective-permute-start.1 = (bf16[512,512]{1,0:T(8,128)(2,1)S(1)}, bf16[512,512]{1,0:T(8,128)(2,1)}, u32[]{:S(2)}, u32[]{:S(2)}) collective-permute-start(bf16[512,512]{1,0:T(8,128)(2,1)S(1)} %slice.119), channel_id=1, source_target_pairs={{0,8},{8,16},{16,24},{24,32},{32,40},{40,48},{48,56},{56,64},{64,7... | collective-permute-start | bytes 1572872 | tf_op jit(solution)/shard_map/ppermute | solution.py:21
  373.4 20.7 %collective-permute-start.2 = (bf16[512,512]{1,0:T(8,128)(2,1)}, bf16[512,512]{1,0:T(8,128)(2,1)}, u32[]{:S(2)}, u32[]{:S(2)}) collective-permute-start(bf16[512,512]{1,0:T(8,128)(2,1)} %collective-permute-done.1), channel_id=1, source_target_pairs={{0,8},{8,16},{16,24},{24,32},{32,40},{40,48},{48,56},{56,64},{64,7... | collective-permute-start | bytes 1572872 | tf_op jit(solution)/shard_map/ppermute | solution.py:21
  396.1 3.0 copy-start.2
  400.4 1.0 copy-start.4
Sparse Core Ops, SparseCore 0:
  181.4 92.3 all-gather.2
  276.8 71.4 all-gather.4
where the time goes:
time: 411 us; the launch traced here: 410 us
  waiting for transfers between devices  203 us (49%)
  other arithmetic  94.5 us (23%)
  matrix products  34.9 us (8%)
  local copies, waits for them, and re-layouts  23.4 us (6%)
  blocking collectives  21.9 us (5%)
  starting transfers between devices  17.3 us (4%)
  between operations  14.4 us (4%)
    all_gather x1, waiting for transfers between devices, on_device(): gathered = lax.all_gather(mixer, 'tp', axis=1, tiled=True)  89.4 us
    add x16, other arithmetic, add_mode(): return running + term  78.5 us
    all_gather x1, waiting for transfers between devices, on_device(): shard_rows = lax.all_gather(qkv_weight, 'ctx', axis=0, tiled=True)  71.4 us
    ppermute x3, waiting for transfers between devices, from_behind(): lax.ppermute(value, axis, [(source, source + steps) for source in range(l...  28.8 us
    all_to_all x1, blocking collectives, on_device(): lax.all_to_all(filtered, 'ctx', split_axis=1, concat_axis=0, tiled=True)  21.9 us
    dot_general x1, matrix products, channel_conv(): entering = jnp.einsum('cnkb,cnb->cnk', carry, block_ends, precision=PRECISE)  14.1 us
    all_to_all x1, waiting for transfers between devices, on_device(): lax.all_to_all(gated.T, 'ctx', split_axis=0, concat_axis=1, tiled=True)  13.6 us
    all_to_all x1, starting transfers between devices, on_device(): lax.all_to_all(gated.T, 'ctx', split_axis=0, concat_axis=1, tiled=True)  10.8 us
  transfers between devices with their start and end apart: 6, of which 5 were waited for; matrix products, arithmetic and copies ran while one was open for 24% of the time, Pallas kernels for 0%

commit v1 on v0

v1 whole, which is shorter than its diff:
```python
from functools import reduce
import math

import jax
import jax.numpy as jnp
from jax import lax
from jax.sharding import PartitionSpec as P

HD = 128
TAPS = 7
WINDOW = 3
CHUNK = 128


EPSILON = 1e-06
PRECISE = lax.Precision.HIGHEST


def to_bf16_grid(value):
    return lax.reduce_precision(value, exponent_bits=8, mantissa_bits=7)


def from_behind(value, axis, steps):
    count = lax.axis_size(axis)
    leading, last = (max(0, -steps), min(count, count - steps))
    return lax.ppermute(value, axis, [(source, source + steps) for source in range(leading, last)])


def local_modal_conv(signal, decay, mixing):
    tokens, channels = signal.shape
    modes = decay.shape[0]
    chunks = tokens // CHUNK
    centre = (CHUNK - 1) / 2.0
    offsets = jnp.arange(CHUNK, dtype=jnp.float32) - centre
    up = jnp.exp(offsets[:, None, None] * decay[None])
    down = jnp.exp(-offsets[:, None, None] * decay[None])
    after = jnp.exp(-(jnp.arange(CHUNK, dtype=jnp.float32) + 1.0)[:, None, None] * decay[None])
    tri = (jnp.arange(CHUNK)[:, None] >= jnp.arange(CHUNK)[None, :]).astype(jnp.float32)
    blocks = signal.reshape(chunks, CHUNK, channels)
    lifted = (up[None] * blocks[:, :, None, :]).reshape(chunks, CHUNK, modes * channels)
    summed = jnp.einsum("ts,qsk->qtk", tri, lifted, precision=PRECISE).reshape(chunks, CHUNK, modes, channels)
    states = down[None] * summed
    intra = jnp.sum(states * mixing[None, None], axis=2)
    ends = states[:, CHUNK - 1]
    step = jnp.exp(-float(CHUNK) * decay)
    carry = jnp.zeros_like(decay)
    entering = []
    for chunk in range(chunks):
        entering.append(carry)
        carry = step * carry + ends[chunk]
    entering = jnp.stack(entering)
    weighted_after = after * mixing[None]
    return intra, entering, carry, weighted_after


def on_device(features, short_filter, decay_rate, residue, skip_gain, norm_gain, qkv_weight):
    tok_dev, _, channels = features.shape
    head_cols = qkv_weight.shape[2]
    shard_rows = lax.all_gather(qkv_weight, "ctx", axis=0, tiled=True)
    rim_rows = features[tok_dev - (TAPS - 1) :]
    before = from_behind(rim_rows, "ctx", 1)
    extended = jnp.concatenate([before, features], axis=0).astype(jnp.float32)
    short_conv = jnp.zeros((tok_dev, 3, channels), jnp.float32)
    for offset in range(TAPS):
        first_row = TAPS - 1 - offset
        short_conv = (
            short_conv
            + short_filter[:, offset, :][None] * extended[first_row : first_row + tok_dev]
        )
    gated = to_bf16_grid(short_conv[:, 1] * short_conv[:, 2])

    mixing = residue * jnp.sqrt(decay_rate)
    intra, entering, block_end, weighted_after = local_modal_conv(gated, decay_rate, mixing)

    block_step = jnp.exp(-float(tok_dev) * decay_rate)
    history = from_behind(block_end, "ctx", 1)
    factor = block_step
    count = lax.axis_size("ctx")
    shift = 1
    while shift < count:
        history = history + factor * from_behind(history, "ctx", shift)
        factor = factor * factor
        shift *= 2

    chunks = tok_dev // CHUNK
    chunk_step = jnp.exp(-float(CHUNK) * decay_rate)
    lead = [jnp.ones_like(decay_rate)]
    for chunk in range(1, chunks):
        lead.append(lead[-1] * chunk_step)
    lead = jnp.stack(lead)
    total_state = entering + lead * history[None]
    carried = jnp.einsum("lnc,qnc->qlc", weighted_after, total_state, precision=PRECISE)
    filtered = (intra + carried).reshape(tok_dev, channels) + skip_gain[None] * gated
    filtered = to_bf16_grid(filtered)
    mixer = (short_conv[:, 0] * filtered).astype(jnp.bfloat16)

    gathered = lax.all_gather(mixer, "tp", axis=1, tiled=True)
    as_float = gathered.astype(jnp.float32)
    inverse = lax.rsqrt(jnp.mean(as_float * as_float, axis=1, keepdims=True) + EPSILON)
    normed = (as_float * inverse * norm_gain[None]).astype(jnp.bfloat16)
    flat_rows = shard_rows.reshape(shard_rows.shape[0], 3 * head_cols)
    projected = jnp.dot(normed, flat_rows, preferred_element_type=jnp.float32).astype(jnp.bfloat16)
    heads = head_cols // HD
    query = projected[:, :head_cols].reshape(tok_dev, heads, HD)
    kv_pair = projected[:, head_cols:]
    blocks_kv = [kv_pair] + [from_behind(kv_pair, "ctx", lag) for lag in range(1, WINDOW)]
    position = lax.axis_index("ctx")
    row_ids = jnp.arange(tok_dev)
    causal = row_ids[:, None] >= row_ids[None, :]
    score_list = []
    for lag_step in range(WINDOW):
        keys = blocks_kv[lag_step][:, :head_cols].reshape(tok_dev, heads, HD)
        scores = jnp.einsum(
            "thd,shd->hts", query, keys, preferred_element_type=jnp.float32
        ) / math.sqrt(HD)
        if lag_step == 0:
            allowed = causal
        else:
            allowed = jnp.broadcast_to(position >= lag_step, causal.shape)
        score_list.append(jnp.where(allowed[None], scores, -jnp.inf))
    peak = reduce(jnp.maximum, [jnp.max(entry, axis=2) for entry in score_list])
    total = jnp.zeros((heads, tok_dev), jnp.float32)
    output = jnp.zeros((tok_dev, heads, HD), jnp.float32)
    for lag_step in range(WINDOW):
        expo = jnp.exp(score_list[lag_step] - peak[:, :, None])
        total = total + jnp.sum(expo, axis=2)
        values = blocks_kv[lag_step][:, head_cols:].reshape(tok_dev, heads, HD)
        output = output + jnp.einsum(
            "hts,shd->thd", expo.astype(jnp.bfloat16), values, preferred_element_type=jnp.float32
        )
    attended = (output / total.T[:, :, None]).astype(jnp.bfloat16).reshape(tok_dev, head_cols)
    return (mixer, attended)


def solution(mesh):
    placed = (
        P("ctx", None, "tp"),
        P(None, None, "tp"),
        P(None, "tp"),
        P(None, "tp"),
        P("tp"),
        P(),
        P("ctx", None, "tp"),
    )
    return jax.shard_map(
        on_device,
        mesh=mesh,
        in_specs=placed,
        out_specs=(P("ctx", "tp"), P("ctx", "tp")),
        check_vma=False,
    )
```

time: 411 us -> 398 us (0.968)
  the two profiles are of different devices: /device:TPU:128 before, /device:TPU:105 now
where the time goes in v1:
time: 398 us; the launch traced here: 397 us
  waiting for transfers between devices  222 us (56%)
  local copies, waits for them, and re-layouts  44.1 us (11%)
  other arithmetic  43.3 us (11%)
  starting transfers between devices  37.1 us (9%)
  matrix products  35.9 us (9%)
  between operations  14.3 us (4%)
    all_gather x1, waiting for transfers between devices, on_device(): gathered = lax.all_gather(mixer, 'tp', axis=1, tiled=True)  102 us
    all_gather x1, waiting for transfers between devices, on_device(): shard_rows = lax.all_gather(qkv_weight, 'ctx', axis=0, tiled=True)  74.5 us
    ppermute x9, waiting for transfers between devices, from_behind(): lax.ppermute(value, axis, [(source, source + steps) for source in range(l...  45.3 us
    ppermute x9, starting transfers between devices, from_behind(): lax.ppermute(value, axis, [(source, source + steps) for source in range(l...  37 us
    reshape x1, local copies, waits for them, and re-layouts, local_modal_conv(): jnp.einsum('ts,qsk->qtk', tri, lifted, precision=PRECISE)  19.9 us
    dot_general x1, matrix products, local_modal_conv(): jnp.einsum('ts,qsk->qtk', tri, lifted, precision=PRECISE)  14.5 us
    reduce_sum x1, other arithmetic, local_modal_conv(): intra = jnp.sum(states * mixing[None, None], axis=2)  10.5 us
    mul x1, other arithmetic, local_modal_conv(): up[None] * blocks[:, :, None, :]  9.46 us
  transfers between devices with their start and end apart: 11, of which 9 were waited for; matrix products, arithmetic and copies ran while one was open for 7% of the time, Pallas kernels for 0%

profile of v1, /device:TPU:105, one launch (start us, length us, event | category | flops | bytes accessed | tf_op | source)
XLA Modules:
  0.0 396.7 jit_solution(14588440854774348517)
XLA Ops:
  8.0 3.7 collective-permute-start
  15.3 4.6 %multiply_exponential_fusion = f32[128,8192]{0,1:T(8,128)} fusion(f32[8192]{0:T(1024)S(1)} %bitcast.158, f32[128]{0:T(128)S(1)} %iota_add_fusion), kind=kLoop, calls=%fused_computation.15 | loop fusion | flops 1048576 | bytes 4227584 | tf_op jit(solution)/shard_map/exp | solution.py:35
  19.9 3.6 multiply_exponential_fusion.1
  23.5 5.8 %copy.51 = f32[128,16,512]{2,1,0:T(8,128)} copy(f32[128,16,512]{0,1,2:T(8,128)} %multiply_exponential_fusion.1) | data formatting | bytes 8388608 | tf_op jit(solution)/shard_map/exp | solution.py:36
  36.1 9.5 %bitcast_multiply_fusion = f32[4,128,8192]{1,2,0:T(8,128)} fusion(f32[4,128,512]{1,2,0:T(8,128)} %copy.52, f32[128,8192]{0,1:T(8,128)} %multiply_exponential_fusion), kind=kLoop, calls=%fused_computation | loop fusion | flops 4194304 | bytes 22020096 | tf_op jit(solution)/shard_map/mul | solution.py:40
  45.6 14.5 %fusion.78 = f32[4,8192,128]{2,1,0:T(8,128)} fusion(f32[4,128,8192]{1,2,0:T(8,128)} %bitcast_multiply_fusion), kind=kOutput, calls=%fused_computation.102 | convolution fusion | flops 6442467328 | bytes 33554432 | tf_op jit(solution)/shard_map/ts,qsk->qtk/dot_general | solution.py:41
  60.1 19.9 %copy.53 = f32[4,128,16,512]{3,2,1,0:T(8,128)} copy(f32[4,128,16,512]{1,3,2,0:T(8,128)} %bitcast.151) | data formatting | bytes 33554432 | tf_op jit(solution)/shard_map/reshape | solution.py:41
  80.0 10.5 %multiply_reduce_fusion = (f32[4,128,512]{2,1,0:T(8,128)}, f32[4,128,16,512]{3,2,1,0:T(8,128)S(1)}) fusion(f32[16,512]{1,0:T(8,128)S(1)} %sqrt_multiply_fusion, f32[4,128,16,512]{3,2,1,0:T(8,128)} %copy.53, f32[128,16,512]{2,1,0:T(8,128)} %copy.51), kind=kLoop, calls=%fused_computation.1 | loop fusion | flops 12320768 | bytes 38830080 | tf_op jit(solution)/shard_map/reduce_sum | solution.py:43
  94.2 4.0 %collective-permute-start.2 = (f32[16,512]{1,0:T(8,128)S(1)}, f32[16,512]{1,0:T(8,128)S(1)}, u32[]{:S(2)}, u32[]{:S(2)}) collective-permute-start(f32[16,512]{1,0:T(8,128)S(1)} %collective-permute-done.1), channel_id=1, source_target_pairs={{0,8},{8,16},{16,24},{24,32},{32,40},{40,48},{48,56},{56,64},{64,7... | collective-permute-start | bytes 98312 | tf_op jit(solution)/shard_map/ppermute | solution.py:26
  98.3 2.6 collective-permute-done.2
  103.0 6.0 %collective-permute-done.3 = f32[16,512]{1,0:T(8,128)S(1)} collective-permute-done((f32[16,512]{1,0:T(8,128)S(1)}, f32[16,512]{1,0:T(8,128)S(1)}, u32[]{:S(2)}, u32[]{:S(2)}) %collective-permute-start.3) | collective-permute-done | bytes 32800 | tf_op jit(solution)/shard_map/ppermute | solution.py:26
  109.0 5.1 %collective-permute-start.4 = (f32[16,512]{1,0:T(8,128)S(1)}, f32[16,512]{1,0:T(8,128)S(1)}, u32[]{:S(2)}, u32[]{:S(2)}) collective-permute-start(f32[16,512]{1,0:T(8,128)S(1)} %multiply_add_fusion.3), channel_id=1, source_target_pairs={{0,32},{8,40},{16,48},{24,56},{32,64},{40,72},{48,80},{56,88},{64,... | collective-permute-start | bytes 98312 | tf_op jit(solution)/shard_map/ppermute | solution.py:26
  114.2 2.8 collective-permute-done.4
  117.0 8.7 %collective-permute-start.5 = (f32[16,512]{1,0:T(8,128)S(1)}, f32[16,512]{1,0:T(8,128)S(1)}, u32[]{:S(2)}, u32[]{:S(2)}) collective-permute-start(f32[16,512]{1,0:T(8,128)S(1)} %multiply_add_fusion.2), channel_id=1, source_target_pairs={{0,64},{8,72},{16,80},{24,88},{32,96},{40,104},{48,112},{56,120},{... | collective-permute-start | bytes 98312 | tf_op jit(solution)/shard_map/ppermute | solution.py:26
  126.8 4.9 %collective-permute-start.6 = (f32[16,512]{1,0:T(8,128)S(1)}, f32[16,512]{1,0:T(8,128)}, u32[]{:S(2)}, u32[]{:S(2)}) collective-permute-start(f32[16,512]{1,0:T(8,128)S(1)} %multiply_add_fusion.1), channel_id=1, source_target_pairs={{0,128},{8,136},{16,144},{24,152},{32,160},{40,168},{48,176},{56,1... | collective-permute-start | bytes 98312 | tf_op jit(solution)/shard_map/ppermute | solution.py:26
  139.6 7.4 %fusion.35 = f32[4,128,512]{1,0,2:T(4,128)} fusion(f32[4,128,512]{1,0,2:T(4,128)} %copy.56, f32[4,16,512]{1,0,2:T(4,128)} %copy.55, f32[16,512]{0,1:T(8,128)} %copy.54, f32[128]{0:T(128)S(1)} %add_negate_fusion, f32[16,512]{0,1:T(8,128)S(1)} %copy.50), kind=kOutput, calls=%fused_computation.51 | convolution fusion | flops 52690944 | bytes 2294272 | tf_op jit(solution)/shard_map/lnc,qnc->qlc/dot_general | solution.py:92
  153.2 102.1 %all-gather.3.cloned.1.call-done = bf16[512,4096]{1,0:T(8,128)(2,1)} async-done(((bf16[512,512]{1,0:T(8,128)(2,1)}), bf16[512,4096]{1,0:T(8,128)(2,1)}) %all-gather.3.cloned.1.call-update) | async-done | bytes 4194320 | tf_op jit(solution)/shard_map/all_gather | solution.py:97
  255.4 3.1 fusion
  258.5 74.5 %all-gather.5.cloned.1.call-done = bf16[4096,3,256]{0,2,1:T(8,128)(2,1)} async-done(((bf16[128,3,256]{0,2,1:T(8,128)(2,1)}), bf16[4096,3,256]{0,2,1:T(8,128)(2,1)}) %all-gather.5.cloned.1.call-update) | async-done | bytes 6291472 | tf_op jit(solution)/shard_map/all_gather | solution.py:59
  332.9 7.5 %fusion.29 = bf16[512,768]{1,0:T(8,128)(2,1)S(1)} fusion(bf16[4096,768]{0,1:T(8,128)(2,1)} %bitcast.160, bf16[512,4096]{1,0:T(8,128)(2,1)} %all-gather.3.cloned.1.call-done, f32[4096]{0:T(1024)S(1)} %copy-done.6, f32[512]{0:T(512)S(1)} %add_rsqrt_fusion), kind=kOutput, calls=%fused_computation.49 | convolution fusion | flops 3230007296 | bytes 11290624 | tf_op jit(solution)/shard_map/dot_general | solution.py:102
  340.5 3.2 collective-permute-start.7
  343.8 3.3 collective-permute-start.8
  349.9 2.8 collective-permute-done.7
  352.9 28.8 %collective-permute-done.8 = bf16[512,512]{1,0:T(8,128)(2,1)S(1)} collective-permute-done((bf16[512,512]{1,0:T(8,128)(2,1)S(1)}, bf16[512,512]{1,0:T(8,128)(2,1)S(1)}, u32[]{:S(2)}, u32[]{:S(2)}) %collective-permute-start.8) | collective-permute-done | bytes 524320 | tf_op jit(solution)/shard_map/ppermute | solution.py:26
  (74 shorter events, 43.3 us)
Async XLA Ops:
  7.2 248.2 %all-gather.3.cloned.1.call-start = ((), (), s32[]{:S(2)}) async-start(), calls=%async_computation | async-start | bytes 4718592 | tf_op jit(solution)/shard_map/all_gather | solution.py:97
  8.0 21.4 %collective-permute-start = (bf16[6,3,512]{2,0,1:T(8,128)(2,1)S(1)}, bf16[6,3,512]{2,0,1:T(8,128)(2,1)S(1)}, u32[]{:S(2)}, u32[]{:S(2)}) collective-permute-start(bf16[6,3,512]{2,0,1:T(8,128)(2,1)S(1)} %slice.102), channel_id=1, source_target_pairs={{0,8},{8,16},{16,24},{24,32},{32,40},{40,48},{48,56},{56,64},{64,7... | collective-permute-start | bytes 55304 | tf_op jit(solution)/shard_map/ppermute | solution.py:26
  23.5 5.8 %copy-start.2 = (bf16[512,3,512]{2,0,1:T(8,128)(2,1)S(1)}, bf16[512,3,512]{2,0,1:T(8,128)(2,1)}, u32[]{:S(2)}) copy-start(bf16[512,3,512]{2,0,1:T(8,128)(2,1)} %param.7) | copy-start | bytes 4718596
  80.0 10.5 %copy-start = (f32[16,512]{1,0:T(8,128)S(1)}, f32[16,512]{1,0:T(8,128)}, u32[]{:S(2)}) copy-start(f32[16,512]{1,0:T(8,128)} %param.9) | copy-start | bytes 98308
  91.1 3.1 collective-permute-start.1
  94.2 6.6 %collective-permute-start.2 = (f32[16,512]{1,0:T(8,128)S(1)}, f32[16,512]{1,0:T(8,128)S(1)}, u32[]{:S(2)}, u32[]{:S(2)}) collective-permute-start(f32[16,512]{1,0:T(8,128)S(1)} %collective-permute-done.1), channel_id=1, source_target_pairs={{0,8},{8,16},{16,24},{24,32},{32,40},{40,48},{48,56},{56,64},{64,7... | collective-permute-start | bytes 98312 | tf_op jit(solution)/shard_map/ppermute | solution.py:26
  100.9 8.2 %collective-permute-start.3 = (f32[16,512]{1,0:T(8,128)S(1)}, f32[16,512]{1,0:T(8,128)S(1)}, u32[]{:S(2)}, u32[]{:S(2)}) collective-permute-start(f32[16,512]{1,0:T(8,128)S(1)} %multiply_add_fusion.4), channel_id=1, source_target_pairs={{0,16},{8,24},{16,32},{24,40},{32,48},{40,56},{48,64},{56,72},{64,... | collective-permute-start | bytes 98312 | tf_op jit(solution)/shard_map/ppermute | solution.py:26
  109.0 8.0 %collective-permute-start.4 = (f32[16,512]{1,0:T(8,128)S(1)}, f32[16,512]{1,0:T(8,128)S(1)}, u32[]{:S(2)}, u32[]{:S(2)}) collective-permute-start(f32[16,512]{1,0:T(8,128)S(1)} %multiply_add_fusion.3), channel_id=1, source_target_pairs={{0,32},{8,40},{16,48},{24,56},{32,64},{40,72},{48,80},{56,88},{64,... | collective-permute-start | bytes 98312 | tf_op jit(solution)/shard_map/ppermute | solution.py:26
  117.0 9.8 %collective-permute-start.5 = (f32[16,512]{1,0:T(8,128)S(1)}, f32[16,512]{1,0:T(8,128)S(1)}, u32[]{:S(2)}, u32[]{:S(2)}) collective-permute-start(f32[16,512]{1,0:T(8,128)S(1)} %multiply_add_fusion.2), channel_id=1, source_target_pairs={{0,64},{8,72},{16,80},{24,88},{32,96},{40,104},{48,112},{56,120},{... | collective-permute-start | bytes 98312 | tf_op jit(solution)/shard_map/ppermute | solution.py:26
  126.8 8.3 %collective-permute-start.6 = (f32[16,512]{1,0:T(8,128)S(1)}, f32[16,512]{1,0:T(8,128)}, u32[]{:S(2)}, u32[]{:S(2)}) collective-permute-start(f32[16,512]{1,0:T(8,128)S(1)} %multiply_add_fusion.1), channel_id=1, source_target_pairs={{0,128},{8,136},{16,144},{24,152},{32,160},{40,168},{48,176},{56,1... | collective-permute-start | bytes 98312 | tf_op jit(solution)/shard_map/ppermute | solution.py:26
  139.6 10.0 %copy-start.5 = (f32[512]{0:T(512)S(1)}, f32[512]{0:T(512)}, u32[]{:S(2)}) copy-start(f32[512]{0:T(512)} %param.11) | copy-start | bytes 6148
  149.6 2.7 copy-start.4
  152.2 180.7 %copy-start.6 = (f32[4096]{0:T(1024)S(1)}, f32[4096]{0:T(1024)}, u32[]{:S(2)}) copy-start(f32[4096]{0:T(1024)} %param.12) | copy-start | bytes 49156
  152.2 180.7 %all-gather.5.cloned.1.call-start = ((), (), s32[]{:S(2)}) async-start(), calls=%async_computation.1 | async-start | bytes 6488064 | tf_op jit(solution)/shard_map/all_gather | solution.py:59
  340.5 12.2 %collective-permute-start.7 = (bf16[512,512]{1,0:T(8,128)(2,1)S(1)}, bf16[512,512]{1,0:T(8,128)(2,1)S(1)}, u32[]{:S(2)}, u32[]{:S(2)}) collective-permute-start(bf16[512,512]{1,0:T(8,128)(2,1)S(1)} %slice.148), channel_id=1, source_target_pairs={{0,8},{8,16},{16,24},{24,32},{32,40},{40,48},{48,56},{56,64},{64,7... | collective-permute-start | bytes 1572872 | tf_op jit(solution)/shard_map/ppermute | solution.py:26
  343.8 38.0 %collective-permute-start.8 = (bf16[512,512]{1,0:T(8,128)(2,1)S(1)}, bf16[512,512]{1,0:T(8,128)(2,1)S(1)}, u32[]{:S(2)}, u32[]{:S(2)}) collective-permute-start(bf16[512,512]{1,0:T(8,128)(2,1)S(1)} %slice.148), channel_id=1, source_target_pairs={{0,16},{8,24},{16,32},{24,40},{32,48},{40,56},{48,64},{56,72},{64,... | collective-permute-start | bytes 1572872 | tf_op jit(solution)/shard_map/ppermute | solution.py:26
  383.1 3.0 copy-start.1
  387.4 1.0 copy-start.3
Sparse Core Ops, SparseCore 0:
  152.4 102.9 all-gather.2
  258.4 74.4 all-gather.4
